TPU v7x, 32 devices: a whole 2x2x4 slice. The times are simulated.
32 devices in a mesh: gx: 2 (over y), gy: 4 (over x, core), gz: 4 (over z).
Axes of the slice: x: 2, y: 2, z: 4, core: 2. Of those that a mesh axis runs over, the one named last changes fastest.
Arguments:
- velocity: float32 [3, 20, 80, 2560], P(None, 'gx', 'gy', 'gz'), may hold values from -6 to 6
- obstacle_element_mask: int32 [4, 16, 512], P('gx', 'gy', 'gz'), may hold values 0 or 1
- element_metric_scale: float32 [4, 16, 512], P('gx', 'gy', 'gz'), may hold values from 0.5 to 8
Outputs:
- smoothed: float32 [20, 80, 2560], P('gx', 'gy', 'gz')
- coarse: float32 [4, 16, 512], P('gx', 'gy', 'gz')
All inputs are finite; a program needn't handle non-finite values. No bound on the sum of `obstacle_element_mask` on one device may be relied on, other than what follows from the above.
Results may differ from a plain program's by a relative error of at most 0.00012.
Values sent between devices are 32-bit elements; how exact they have to be, the bound alone decides.
A program may use at most 384 MiB of HBM per device.

v0:
```python
import functools
import itertools
import math

import jax
import jax.numpy as jnp
import numpy as np
from jax import lax
from jax.experimental import pallas as pl
from jax.experimental.pallas import tpu as pltpu
from jax.sharding import PartitionSpec as P

lift_factor = 10.0
time_step = 0.05
penalty = 4.0
half_lift = lift_factor * 0.5
order = 5
names = ("gx", "gy", "gz")
corners = [s for s in itertools.product((0, 1), repeat=3) if any(s)]


def lobatto_points():
    return np.array([-1.0, -math.sqrt(3.0 / 7.0), 0.0, math.sqrt(3.0 / 7.0), 1.0])


def lobatto_weights():
    return np.array([0.1, 49.0 / 90.0, 32.0 / 45.0, 49.0 / 90.0, 0.1])


def derivative_matrix():
    points = lobatto_points()
    scales = np.array(
        [np.prod([points[i] - points[k] for k in range(5) if k != i]) for i in range(5)]
    )
    result = np.zeros((5, 5))
    for i in range(5):
        for j in range(5):
            if i != j:
                result[i, j] = scales[i] / (scales[j] * (points[i] - points[j]))
        result[i, i] = -np.sum(result[i])
    return result


def eigen_basis_table():
    return np.array(
        [
            [
                math.sqrt((1.0 if k == 0 else 2.0) / 5.0) * math.cos(math.pi * (i + 0.5) * k / 5.0)
                for k in range(5)
            ]
            for i in range(5)
        ]
    )


def eigen_value_table():
    return np.array([4.0 * math.sin(math.pi * k / 10.0) ** 2 for k in range(5)])


def hat_weight_table():
    points = lobatto_points()
    weights = lobatto_weights()
    return np.array([weights * (1.0 - points) / 2.0, weights * (1.0 + points) / 2.0])


def mix(coefs, terms):
    total = None
    for coef, term in zip(coefs, terms):
        if abs(coef) < 1e-12:
            continue
        piece = float(coef) * term
        total = piece if total is None else total + piece
    return total


def lifted_derivative(f):
    d = derivative_matrix()
    d[0, 0] += half_lift
    d[4, 4] -= half_lift
    e1, e2 = f[0] + f[4], f[1] + f[3]
    o1, o2 = f[0] - f[4], f[1] - f[3]
    out = [None] * 5
    for i in range(2):
        even = mix(((d[i, 0] + d[i, 4]) / 2, (d[i, 1] + d[i, 3]) / 2, d[i, 2]), (e1, e2, f[2]))
        odd = mix(((d[i, 0] - d[i, 4]) / 2, (d[i, 1] - d[i, 3]) / 2), (o1, o2))
        out[i] = odd + even
        out[4 - i] = odd - even
    out[2] = mix((d[2, 0], d[2, 1]), (o1, o2))
    return out


def to_modes(f):
    s = eigen_basis_table()
    e1, e2 = f[0] + f[4], f[1] + f[3]
    o1, o2 = f[0] - f[4], f[1] - f[3]
    out = []
    for k in range(5):
        if k == 0:
            out.append(float(s[0, 0]) * (e1 + e2 + f[2]))
        elif k % 2 == 0:
            out.append(mix((s[0, k], s[1, k], s[2, k]), (e1, e2, f[2])))
        else:
            out.append(mix((s[0, k], s[1, k]), (o1, o2)))
    return out


def from_modes(c):
    s = eigen_basis_table()
    out = [None] * 5
    base = float(s[0, 0]) * c[0]
    for i in range(2):
        even = base + mix((s[i, 2], s[i, 4]), (c[2], c[4]))
        odd = mix((s[i, 1], s[i, 3]), (c[1], c[3]))
        out[i] = even + odd
        out[4 - i] = even - odd
    out[2] = base + mix((s[2, 2], s[2, 4]), (c[2], c[4]))
    return out


def at_line(a, l, m):
    return ((l, m), (m, l), (m, slice(None), l))[a]


def roll(x, shift, axis):
    size = x.shape[axis]
    shift = shift % size
    return x if shift == 0 else pltpu.roll(x, shift, axis)


class Brick:
    def __init__(self, ex, ey, ez):
        self.ex, self.ey, self.ez = ex, ey, ez
        self.rows = ex * ey

    def iotas(self):
        row = lax.broadcasted_iota(jnp.int32, (self.rows, self.ez), 0)
        lane = lax.broadcasted_iota(jnp.int32, (self.rows, self.ez), 1)
        return row, lane

    def slots(self, a):
        return (self.ex, self.ey, self.ez)[a]

    def packed(self, a, n):
        return -(-n // self.slots(a))

    def step(self, a):
        return (self.ey, 1, 1)[a]

    def place(self, a):
        row, lane = self.iotas()
        return (row // self.ey, row % self.ey, lane)[a]

    def pack(self, face, a, up):
        n = face.shape[0]
        slots, step = self.slots(a), self.step(a)
        axis = 2 if a == 2 else 1
        place = self.place(a)
        start = slots - 1 if up else 0
        groups = []
        if a == 2:
            total = jnp.zeros((self.rows, self.ez), jnp.float32)
            for s in range(n):
                total = jnp.where(place == s, roll(face[s], s - start, 1), total)
            return total[None]
        for g in range(self.packed(a, n)):
            total = None
            for s in range(min(slots, n - g * slots)):
                piece = roll(face[g * slots + s], (s - start) * step, 0)
                total = piece if total is None else jnp.where(place == s, piece, total)
            groups.append(total)
        return jnp.stack(groups)

    def entry(self, packed_ref, n, a, up):
        slots, step = self.slots(a), self.step(a)
        target = 0 if up else slots - 1
        g, s = divmod(n, slots)
        return roll(packed_ref[g], (target - s) * step, 1 if a == 2 else 0)

    def move(self, x, a, up):
        step = self.step(a) if up else -self.step(a)
        return roll(x, step, 1 if a == 2 else 0)

    def edge(self, a, up):
        return self.place(a) == (0 if up else self.slots(a) - 1)


def body(
    brick,
    counts,
    v_ref,
    mask_ref,
    scale_ref,
    smooth_ref,
    coarse_ref,
    rows_buf,
    vel,
    conv,
    near,
    pres,
    *rest,
):
    send1, recv1, send2, recv2 = rest[0:6], rest[6:12], rest[12:18], rest[18:24]
    send3, recv3 = rest[24], rest[25]
    ssem1, rsem1, ssem2, rsem2, ssem3, rsem3 = rest[26:32]
    ex, ey, ez = brick.ex, brick.ey, brick.ez
    ny = ey * order
    me = [lax.axis_index(name) for name in names]

    def offset_id(shift):
        return tuple(me[a] + shift[a] for a in range(3))

    def exists(shift):
        ok = None
        for a in range(3):
            if shift[a] > 0:
                one = me[a] < counts[a] - 1
            elif shift[a] < 0:
                one = me[a] > 0
            else:
                continue
            ok = one if ok is None else jnp.logical_and(ok, one)
        return ok

    unit = [tuple(int(a == b) for b in range(3)) for a in range(3)]
    partners = [s for s in corners] + [tuple(-x for x in s) for s in corners]
    barrier = pltpu.get_barrier_semaphore()
    for shift in partners:

        @pl.when(exists(shift))
        def _():
            pl.semaphore_signal(
                barrier,
                inc=1,
                device_id=offset_id(shift),
                device_id_type=pl.DeviceIdType.MESH,
            )

    def copies(send, recv, ssem, rsem):
        out = []
        for a in range(3):
            for s in range(2):
                d = 2 * a + s
                sign = 1 - 2 * s
                to = tuple(sign * u for u in unit[a])
                source = tuple(-sign * u for u in unit[a])
                copy = pltpu.make_async_remote_copy(
                    src_ref=send[d],
                    dst_ref=recv[d],
                    send_sem=ssem.at[d],
                    recv_sem=rsem.at[d],
                    device_id=offset_id(to),
                    device_id_type=pl.DeviceIdType.MESH,
                )
                out.append((copy, exists(to), exists(source), recv[d]))
        return out

    def start(group):
        for copy, has_to, has_source, _ in group:

            @pl.when(has_to)
            def _():
                copy.start()

    def clear(group):
        for _, _, has_source, dst in group:

            @pl.when(jnp.logical_not(has_source))
            def _():
                dst[...] = jnp.zeros_like(dst)

    def arrive(group):
        for copy, has_to, has_source, _ in group:

            @pl.when(has_source)
            def _():
                copy.wait_recv()

    def finish(group):
        for copy, has_to, has_source, _ in group:

            @pl.when(has_to)
            def _():
                copy.wait_send()

    round1 = copies(send1, recv1, ssem1, rsem1)
    round2 = copies(send2, recv2, ssem2, rsem2)
    round3 = []
    for n, shift in enumerate(corners):
        copy = pltpu.make_async_remote_copy(
            src_ref=send3.at[n],
            dst_ref=recv3.at[n],
            send_sem=ssem3.at[n],
            recv_sem=rsem3.at[n],
            device_id=offset_id(shift),
            device_id_type=pl.DeviceIdType.MESH,
        )
        back = tuple(-x for x in shift)
        round3.append((copy, exists(shift), exists(back), recv3.at[n]))

    row, lane = brick.iotas()
    spread = pow(order, -1, ez)
    gather_index = (lane * order) % ez
    scatter_index = (lane * spread) % ez

    def permute(x, index):
        return jnp.take_along_axis(x, index, axis=1, mode="promise_in_bounds")

    tile_of = [(((lane - spread * k) % ez) * order + k) // ez for k in range(order)]

    def split(i, carry):
        for c in range(3):
            for t in range(order):
                for x in range(ex):
                    rows_buf[c, i, t, x * ny : (x + 1) * ny, :] = v_ref[
                        c, x * order + i, :, t * ez : (t + 1) * ez
                    ]
            for j in range(order):
                parts = [
                    permute(rows_buf[c, i, t, pl.ds(j, brick.rows, stride=order), :], gather_index)
                    for t in range(order)
                ]
                for k in range(order):
                    total = parts[0]
                    for t in range(1, order):
                        total = jnp.where(tile_of[k] == t, parts[t], total)
                    vel[c, i, j, k] = roll(total, -spread * k, 1)
        return carry

    lax.fori_loop(0, order, split, 0)

    clear(round1)
    clear(round2)
    clear(round3)
    faces = order * order

    def face_of(ref, a, l):
        index = ((l,), (slice(None), l), (slice(None), slice(None), l))[a]
        return ref[index]

    for a in range(3):
        for s in range(2):
            l = order - 1 if s == 0 else 0
            face = jnp.concatenate(
                [
                    face_of(vel.at[c], a, l).reshape(faces, brick.rows, ez)
                    for c in range(3)
                ]
            )
            send1[2 * a + s][...] = brick.pack(face, a, s == 0)

    pl.semaphore_wait(barrier, sum(exists(shift).astype(jnp.int32) for shift in partners))

    start(round1)

    def inner_axis(a):
        def run(m, carry):
            normal = [vel[(a,) + at_line(a, l, m)] for l in range(order)]
            for c in range(3):
                if c == a:
                    flux = [x * x for x in normal]
                else:
                    flux = [normal[l] * vel[(c,) + at_line(a, l, m)] for l in range(order)]
                out = lifted_derivative(flux)
                for l in range(order):
                    where = (c,) + at_line(a, l, m)
                    conv[where] = out[l] if a == 0 else conv[where] + out[l]
            return carry

        lax.fori_loop(0, order, run, 0)

    for a in range(3):
        inner_axis(a)

    arrive(round1)

    for a in range(3):
        for s in range(2):
            up = s == 0
            edge = brick.edge(a, up)
            own, other = (0, order - 1) if up else (order - 1, 0)
            for c in range(3):
                for m in range(order):
                    line = vel[(c,) + at_line(a, other, m)]
                    for q in range(order):
                        n = (c * order + m) * order + q
                        far = brick.entry(recv1[2 * a + s], n, a, up)
                        near[c, m, q] = jnp.where(edge, far, brick.move(line[q], a, up))

            def add_faces(m, carry):
                normal = vel[(a,) + at_line(a, own, m)]
                normal_out = near[a, m]
                speed = jnp.maximum(jnp.abs(normal), jnp.abs(normal_out))
                for c in range(3):
                    moved = vel[(c,) + at_line(a, own, m)]
                    moved_out = near[c, m]
                    jump = speed * (moved_out - moved)
                    flux = normal_out * moved_out
                    where = (c,) + at_line(a, own, m)
                    if up:
                        conv[where] = conv[where] - half_lift * (flux + jump)
                    else:
                        conv[where] = conv[where] + half_lift * (flux - jump)
                return carry

            lax.fori_loop(0, order, add_faces, 0)

    solid = jnp.concatenate([mask_ref[x] for x in range(ex)], axis=0).astype(jnp.float32)
    scale = jnp.concatenate([scale_ref[x] for x in range(ex)], axis=0)
    fluid = 1.0 / (1.0 + penalty * solid)

    def advance(i, carry):
        for c in range(3):
            conv[c, i] = (vel[c, i] - time_step * conv[c, i]) * fluid
        return carry

    lax.fori_loop(0, order, advance, 0)

    for a in range(3):
        for s in range(2):
            l = order - 1 if s == 0 else 0
            face = face_of(conv.at[a], a, l).reshape(faces, brick.rows, ez)
            send2[2 * a + s][...] = brick.pack(face, a, s == 0)
    start(round2)

    for a in range(3):

        def diverge(m, carry):
            out = lifted_derivative([conv[(a,) + at_line(a, l, m)] for l in range(order)])
            for l in range(order):
                where = at_line(a, l, m)
                pres[where] = -out[l] if a == 0 else pres[where] - out[l]
            return carry

        lax.fori_loop(0, order, diverge, 0)

    arrive(round2)
    for a in range(3):
        for s in range(2):
            up = s == 0
            edge = brick.edge(a, up)
            own, other = (0, order - 1) if up else (order - 1, 0)
            for m in range(order):
                line = conv[(a,) + at_line(a, other, m)]
                values = []
                for q in range(order):
                    far = brick.entry(recv2[2 * a + s], m * order + q, a, up)
                    values.append(jnp.where(edge, far, brick.move(line[q], a, up)))
                side = jnp.stack(values)
                where = at_line(a, own, m)
                if up:
                    pres[where] = pres[where] + half_lift * side
                else:
                    pres[where] = pres[where] - half_lift * side

    hats = hat_weight_table()
    by_x = []
    for i in range(order):
        slab = [pres[i, j] for j in range(order)]
        along_y = [mix(hats[b], slab) for b in range(2)]
        by_x.append([[mix(hats[c], [along_y[b][k] for k in range(order)]) for c in range(2)] for b in range(2)])
    parts = {
        (a, b, c): mix(hats[a], [by_x[i][b][c] for i in range(order)])
        for a in range(2)
        for b in range(2)
        for c in range(2)
    }
    for a in (2, 1, 0):
        edge = brick.edge(a, True)
        merged = {}
        for key in parts:
            if key[a] == 1:
                continue
            upper = key[:a] + (1,) + key[a + 1 :]
            moved = brick.move(parts[upper], a, True)
            if a == 1:
                swap = roll(parts[upper], 1 - ey, 0)
                moved = jnp.where(edge, swap, moved)
            merged[key] = parts[key] + jnp.where(edge, 0.0, moved)
            merged[upper] = jnp.where(edge, moved, 0.0)
        parts = merged
    for n, shift in enumerate(corners):
        send3[n] = parts[shift]
    start(round3)

    basis_values = eigen_value_table()

    def forward(i, carry):
        slab = to_modes([pres[i, j] for j in range(order)])
        for j in range(order):
            out = to_modes([slab[j][k] for k in range(order)])
            for k in range(order):
                pres[i, j, k] = out[k]
        return carry

    lax.fori_loop(0, order, forward, 0)

    for j in range(order):
        modes = to_modes([pres[i, j] for i in range(order)])
        scaled = []
        for i in range(order):
            denominator = jnp.stack(
                [
                    scale * float(basis_values[i] + basis_values[j] + basis_values[k]) + 1.0
                    for k in range(order)
                ]
            )
            scaled.append(modes[i] / denominator)
        out = from_modes(scaled)
        for i in range(order):
            pres[i, j] = out[i]

    def backward(i, carry):
        slab = from_modes([pres[i, j] for j in range(order)])
        for j in range(order):
            out = from_modes([slab[j][k] for k in range(order)])
            rolled = [roll(out[k], spread * k, 1) for k in range(order)]
            for t in range(order):
                total = rolled[0]
                for k in range(1, order):
                    total = jnp.where(tile_of[k] == t, rolled[k], total)
                rows_buf[0, i, t, pl.ds(j, brick.rows, stride=order), :] = permute(
                    total, scatter_index
                )
        for t in range(order):
            for x in range(ex):
                smooth_ref[x * order + i, :, t * ez : (t + 1) * ez] = rows_buf[
                    0, i, t, x * ny : (x + 1) * ny, :
                ]
        return carry

    lax.fori_loop(0, order, backward, 0)

    arrive(round3)
    total = parts[(0, 0, 0)]
    for n in range(len(corners)):
        total = total + recv3[n]
    for x in range(ex):
        coarse_ref[x] = total[x * ey : (x + 1) * ey]
    finish(round1)
    finish(round2)
    finish(round3)


def shards(counts, velocity, mask, scale):
    ex, ey, ez = mask.shape
    brick = Brick(ex, ey, ez)
    tile = (brick.rows, ez)
    faces = order * order

    def buffers(n):
        return [
            pltpu.VMEM((brick.packed(a, n),) + tile, jnp.float32)
            for a in range(3)
            for _ in range(2)
        ]

    whole = pl.BlockSpec(memory_space=pltpu.VMEM)
    sems = pltpu.SemaphoreType.DMA
    return pl.pallas_call(
        functools.partial(body, brick, counts),
        out_shape=(
            jax.ShapeDtypeStruct(velocity.shape[1:], jnp.float32),
            jax.ShapeDtypeStruct(mask.shape, jnp.float32),
        ),
        in_specs=[whole] * 3,
        out_specs=(whole, whole),
        scratch_shapes=[
            pltpu.VMEM((3, order, order, brick.rows * order, ez), jnp.float32),
            pltpu.VMEM((3, order, order, order) + tile, jnp.float32),
            pltpu.VMEM((3, order, order, order) + tile, jnp.float32),
            pltpu.VMEM((3, order, order) + tile, jnp.float32),
            pltpu.VMEM((order, order, order) + tile, jnp.float32),
        ]
        + buffers(3 * faces)
        + buffers(3 * faces)
        + buffers(faces)
        + buffers(faces)
        + [
            pltpu.VMEM((len(corners),) + tile, jnp.float32),
            pltpu.VMEM((len(corners),) + tile, jnp.float32),
        ]
        + [sems((6,)), sems((6,)), sems((6,)), sems((6,)), sems((7,)), sems((7,))],
        compiler_params=pltpu.CompilerParams(
            collective_id=0, has_side_effects=True, vmem_limit_bytes=40 * 2**20
        ),
    )(velocity, mask, scale)


def solution(mesh):
    counts = tuple(mesh.shape[name] for name in names)
    return jax.shard_map(
        functools.partial(shards, counts),
        mesh=mesh,
        in_specs=(P(None, "gx", "gy", "gz"), P("gx", "gy", "gz"), P("gx", "gy", "gz")),
        out_specs=(P("gx", "gy", "gz"), P("gx", "gy", "gz")),
        check_vma=False,
    )
```

profile of v0, /device:TPU:0, one launch (start us, length us, event | category | flops | bytes accessed | tf_op | source)
XLA Modules:
  0.0 21.5 jit_solution(9360525070821033175)
XLA Ops:
  0.6 0.0 copy-start
  0.6 1.5 %copy-done = f32[3,10,20,640]{3,2,1,0:T(8,128)S(1)} copy-done((f32[3,10,20,640]{3,2,1,0:T(8,128)S(1)}, f32[3,10,20,640]{3,2,1,0:T(8,128)}, u32[]{:S(2)}) %copy-start) | copy-done | bytes 1536024
  2.1 0.0 copy-start.1
  2.1 0.7 %copy-done.1 = s32[2,4,128]{2,1,0:T(4,128)S(1)} copy-done((s32[2,4,128]{2,1,0:T(4,128)S(1)}, s32[2,4,128]{2,1,0:T(4,128)}, u32[]{:S(2)}) %copy-start.1) | copy-done | bytes 4120
  2.8 0.0 copy-start.2
  2.8 0.7 %copy-done.2 = f32[2,4,128]{2,1,0:T(4,128)S(1)} copy-done((f32[2,4,128]{2,1,0:T(4,128)S(1)}, f32[2,4,128]{2,1,0:T(4,128)}, u32[]{:S(2)}) %copy-start.2) | copy-done | bytes 4120
  3.5 16.6 %shard_map.50 = (f32[10,20,640]{2,1,0:T(8,128)S(1)}, f32[2,4,128]{2,1,0:T(4,128)S(1)}) custom-call(f32[3,10,20,640]{3,2,1,0:T(8,128)S(1)} %copy-done, s32[2,4,128]{2,1,0:T(4,128)S(1)} %copy-done.1, f32[2,4,128]{2,1,0:T(4,128)S(1)} %copy-done.2), custom_call_target="tpu_custom_call" | custom-call | tf_op jit(solution)/shard_map/pallas_call | solution.py:559
  20.1 0.8 %copy.7 = f32[10,20,640]{2,1,0:T(8,128)} copy(f32[10,20,640]{2,1,0:T(8,128)S(1)} %get-tuple-element.4) | data formatting | bytes 1024000
  20.9 0.6 %copy.8 = f32[2,4,128]{2,1,0:T(4,128)} copy(f32[2,4,128]{2,1,0:T(4,128)S(1)} %get-tuple-element.5) | data formatting | bytes 8192
Async XLA Ops:
  0.6 1.5 %copy-start = (f32[3,10,20,640]{3,2,1,0:T(8,128)S(1)}, f32[3,10,20,640]{3,2,1,0:T(8,128)}, u32[]{:S(2)}) copy-start(f32[3,10,20,640]{3,2,1,0:T(8,128)} %v_ref.1) | copy-start | bytes 4608004
  2.1 0.7 %copy-start.1 = (s32[2,4,128]{2,1,0:T(4,128)S(1)}, s32[2,4,128]{2,1,0:T(4,128)}, u32[]{:S(2)}) copy-start(s32[2,4,128]{2,1,0:T(4,128)} %mask_ref.1) | copy-start | bytes 12292
  2.8 0.7 %copy-start.2 = (f32[2,4,128]{2,1,0:T(4,128)S(1)}, f32[2,4,128]{2,1,0:T(4,128)}, u32[]{:S(2)}) copy-start(f32[2,4,128]{2,1,0:T(4,128)} %scale_ref.1) | copy-start | bytes 12292
where the time goes:
time: 21.7 us; the launch traced here: 21.5 us
  Pallas kernels  16.6 us (76%)
  local copies, waits for them, and re-layouts  4.29 us (20%)
  between operations  0.65 us (3%)
    pallas_call x1, Pallas kernels, shards(): pl.pallas_call(functools.partial(body, brick, counts), out_shape=(jax.Sha...  16.6 us
    unnamed x8, local copies, waits for them, and re-layouts  4.29 us

commit v1 on v0

--- a/solution.py
+++ b/solution.py
@@ -192,16 +192,23 @@
     scale_ref,
     smooth_ref,
     coarse_ref,
+    raw,
+    mask_buf,
+    scale_buf,
     rows_buf,
     vel,
     conv,
     near,
+    far_x,
     pres,
+    raw_x,
     *rest,
 ):
-    send1, recv1, send2, recv2 = rest[0:6], rest[6:12], rest[12:18], rest[18:24]
-    send3, recv3 = rest[24], rest[25]
-    ssem1, rsem1, ssem2, rsem2, ssem3, rsem3 = rest[26:32]
+    send1, recv1, send2, recv2 = rest[0:4], rest[4:8], rest[8:14], rest[14:20]
+    send3, recv3 = rest[20], rest[21]
+    ssem1, rsem1, ssem2, rsem2, ssem3, rsem3, load_sem, small_sem, ssemx, rsemx = rest[
+        22:32
+    ]
     ex, ey, ez = brick.ex, brick.ey, brick.ez
     ny = ey * order
     me = [lax.axis_index(name) for name in names]
@@ -221,8 +228,17 @@
             ok = one if ok is None else jnp.logical_and(ok, one)
         return ok
 
+    layers = ex * order
+    loads = [
+        pltpu.make_async_copy(v_ref.at[:, n], raw.at[:, n], load_sem.at[n]) for n in range(layers)
+    ]
+    small = [
+        pltpu.make_async_copy(mask_ref, mask_buf, small_sem.at[0]),
+        pltpu.make_async_copy(scale_ref, scale_buf, small_sem.at[1]),
+    ]
+
     unit = [tuple(int(a == b) for b in range(3)) for a in range(3)]
-    partners = [s for s in corners] + [tuple(-x for x in s) for s in corners]
+    partners = unit + [tuple(-x for x in u) for u in unit]
     barrier = pltpu.get_barrier_semaphore()
     for shift in partners:
 
@@ -235,23 +251,30 @@
                 device_id_type=pl.DeviceIdType.MESH,
             )
 
-    def copies(send, recv, ssem, rsem):
+    for i in range(order):
+        for x in range(ex):
+            loads[x * order + i].start()
+    for copy in small:
+        copy.start()
+
+    def transfer(src, dst, ssem, rsem, to):
+        copy = pltpu.make_async_remote_copy(
+            src_ref=src,
+            dst_ref=dst,
+            send_sem=ssem,
+            recv_sem=rsem,
+            device_id=offset_id(to),
+            device_id_type=pl.DeviceIdType.MESH,
+        )
+        return (copy, exists(to), exists(tuple(-x for x in to)), dst)
+
+    def copies(send, recv, ssem, rsem, axes):
         out = []
-        for a in range(3):
+        for n, a in enumerate(axes):
             for s in range(2):
-                d = 2 * a + s
-                sign = 1 - 2 * s
-                to = tuple(sign * u for u in unit[a])
-                source = tuple(-sign * u for u in unit[a])
-                copy = pltpu.make_async_remote_copy(
-                    src_ref=send[d],
-                    dst_ref=recv[d],
-                    send_sem=ssem.at[d],
-                    recv_sem=rsem.at[d],
-                    device_id=offset_id(to),
-                    device_id_type=pl.DeviceIdType.MESH,
-                )
-                out.append((copy, exists(to), exists(source), recv[d]))
+                d = 2 * n + s
+                to = tuple((1 - 2 * s) * u for u in unit[a])
+                out.append(transfer(send[d], recv[d], ssem.at[d], rsem.at[d], to))
         return out
 
     def start(group):
@@ -282,20 +305,20 @@
             def _():
                 copy.wait_send()
 
-    round1 = copies(send1, recv1, ssem1, rsem1)
-    round2 = copies(send2, recv2, ssem2, rsem2)
-    round3 = []
-    for n, shift in enumerate(corners):
-        copy = pltpu.make_async_remote_copy(
-            src_ref=send3.at[n],
-            dst_ref=recv3.at[n],
-            send_sem=ssem3.at[n],
-            recv_sem=rsem3.at[n],
-            device_id=offset_id(shift),
-            device_id_type=pl.DeviceIdType.MESH,
-        )
-        back = tuple(-x for x in shift)
-        round3.append((copy, exists(shift), exists(back), recv3.at[n]))
+    round1x = []
+    for c in range(3):
+        for s, n in enumerate((layers - 1, 0)):
+            to = tuple((1 - 2 * s) * u for u in unit[0])
+            d = 2 * c + s
+            round1x.append(
+                transfer(v_ref.at[c, n], raw_x.at[s, c], ssemx.at[d], rsemx.at[d], to)
+            )
+    round1 = copies(send1, recv1, ssem1, rsem1, (1, 2))
+    round2 = copies(send2, recv2, ssem2, rsem2, (0, 1, 2))
+    round3 = [
+        transfer(send3.at[n], recv3.at[n], ssem3.at[n], rsem3.at[n], shift)
+        for n, shift in enumerate(corners)
+    ]
 
     row, lane = brick.iotas()
     spread = pow(order, -1, ez)
@@ -307,27 +330,42 @@
 
     tile_of = [(((lane - spread * k) % ez) * order + k) // ez for k in range(order)]
 
-    def split(i, carry):
-        for c in range(3):
+    def split_layer(slab, rows, put, components=(0, 1, 2)):
+        for c in components:
             for t in range(order):
-                for x in range(ex):
-                    rows_buf[c, i, t, x * ny : (x + 1) * ny, :] = v_ref[
-                        c, x * order + i, :, t * ez : (t + 1) * ez
-                    ]
+                for x in slab:
+                    rows[c, t, x * ny : (x + 1) * ny, :] = slab[x](c, slice(t * ez, (t + 1) * ez))
             for j in range(order):
                 parts = [
-                    permute(rows_buf[c, i, t, pl.ds(j, brick.rows, stride=order), :], gather_index)
+                    permute(rows[c, t, pl.ds(j, brick.rows, stride=order), :], gather_index)
                     for t in range(order)
                 ]
                 for k in range(order):
                     total = parts[0]
                     for t in range(1, order):
                         total = jnp.where(tile_of[k] == t, parts[t], total)
-                    vel[c, i, j, k] = roll(total, -spread * k, 1)
+                    put(c, j, k, roll(total, -spread * k, 1))
+
+    pl.semaphore_wait(barrier, sum(exists(shift).astype(jnp.int32) for shift in partners))
+    start(round1x)
+
+    def split(i, carry):
+        for x in range(ex):
+            n = x * order + i
+            pltpu.make_async_copy(v_ref.at[:, n], raw.at[:, n], load_sem.at[n]).wait()
+
+        def reader(x):
+            return lambda c, lanes: raw[c, x * order + i, :, lanes]
+
+        def put(c, j, k, value):
+            vel[c, i, j, k] = value
+
+        split_layer({x: reader(x) for x in range(ex)}, rows_buf.at[i], put)
         return carry
 
     lax.fori_loop(0, order, split, 0)
 
+    clear(round1x)
     clear(round1)
     clear(round2)
     clear(round3)
@@ -337,20 +375,14 @@
         index = ((l,), (slice(None), l), (slice(None), slice(None), l))[a]
         return ref[index]
 
-    for a in range(3):
+    for a in (2, 1):
         for s in range(2):
             l = order - 1 if s == 0 else 0
             face = jnp.concatenate(
-                [
-                    face_of(vel.at[c], a, l).reshape(faces, brick.rows, ez)
-                    for c in range(3)
-                ]
+                [face_of(vel.at[c], a, l).reshape(faces, brick.rows, ez) for c in range(3)]
             )
-            send1[2 * a + s][...] = brick.pack(face, a, s == 0)
-
-    pl.semaphore_wait(barrier, sum(exists(shift).astype(jnp.int32) for shift in partners))
-
-    start(round1)
+            send1[2 * (a - 1) + s][...] = brick.pack(face, a, s == 0)
+        start(round1[2 * (a - 1) : 2 * a])
 
     def inner_axis(a):
         def run(m, carry):
@@ -371,28 +403,35 @@
     for a in range(3):
         inner_axis(a)
 
-    arrive(round1)
-
-    for a in range(3):
+    for copy in small:
+        copy.wait()
+    solid = jnp.concatenate([mask_buf[x] for x in range(ex)], axis=0).astype(jnp.float32)
+    scale = jnp.concatenate([scale_buf[x] for x in range(ex)], axis=0)
+    fluid = 1.0 / (1.0 + penalty * solid)
+
+    def face_terms(a, components=(0, 1, 2)):
         for s in range(2):
             up = s == 0
             edge = brick.edge(a, up)
             own, other = (0, order - 1) if up else (order - 1, 0)
-            for c in range(3):
+            for c in components:
                 for m in range(order):
                     line = vel[(c,) + at_line(a, other, m)]
                     for q in range(order):
                         n = (c * order + m) * order + q
-                        far = brick.entry(recv1[2 * a + s], n, a, up)
-                        near[c, m, q] = jnp.where(edge, far, brick.move(line[q], a, up))
+                        if a == 0:
+                            far = far_x[c, m, q]
+                        else:
+                            far = brick.entry(recv1[2 * (a - 1) + s], n, a, up)
+                        near[s, c, m, q] = jnp.where(edge, far, brick.move(line[q], a, up))
 
             def add_faces(m, carry):
                 normal = vel[(a,) + at_line(a, own, m)]
-                normal_out = near[a, m]
+                normal_out = near[s, a, m]
                 speed = jnp.maximum(jnp.abs(normal), jnp.abs(normal_out))
-                for c in range(3):
+                for c in components:
                     moved = vel[(c,) + at_line(a, own, m)]
-                    moved_out = near[c, m]
+                    moved_out = near[s, c, m]
                     jump = speed * (moved_out - moved)
                     flux = normal_out * moved_out
                     where = (c,) + at_line(a, own, m)
@@ -402,27 +441,35 @@
                         conv[where] = conv[where] + half_lift * (flux - jump)
                 return carry
 
-            lax.fori_loop(0, order, add_faces, 0)
-
-    solid = jnp.concatenate([mask_ref[x] for x in range(ex)], axis=0).astype(jnp.float32)
-    scale = jnp.concatenate([scale_ref[x] for x in range(ex)], axis=0)
-    fluid = 1.0 / (1.0 + penalty * solid)
-
-    def advance(i, carry):
-        for c in range(3):
-            conv[c, i] = (vel[c, i] - time_step * conv[c, i]) * fluid
-        return carry
-
-    lax.fori_loop(0, order, advance, 0)
+            lax.fori_loop(0, order, add_faces, 0, unroll=True)
+
+    def advance(c, i):
+        conv[c, i] = (vel[c, i] - time_step * conv[c, i]) * fluid
+
+    for a in (2, 1):
+        arrive(round1[2 * (a - 1) : 2 * a])
+        face_terms(a)
+    for c in range(3):
+        for i in range(1, order - 1):
+            advance(c, i)
+
+    def reader_x(side):
+        return lambda c, lanes: raw_x[side, c, :, lanes]
+
+    def put_x(c, j, k, value):
+        far_x[c, j, k] = value
 
     for a in range(3):
+        arrive(round1x[2 * a : 2 * a + 2])
+        split_layer({0: reader_x(0), ex - 1: reader_x(1)}, rows_buf.at[0], put_x, (a,))
+        face_terms(0, (a,))
+        advance(a, 0)
+        advance(a, order - 1)
         for s in range(2):
             l = order - 1 if s == 0 else 0
             face = face_of(conv.at[a], a, l).reshape(faces, brick.rows, ez)
             send2[2 * a + s][...] = brick.pack(face, a, s == 0)
-    start(round2)
-
-    for a in range(3):
+        start(round2[2 * a : 2 * a + 2])
 
         def diverge(m, carry):
             out = lifted_derivative([conv[(a,) + at_line(a, l, m)] for l in range(order)])
@@ -431,10 +478,10 @@
                 pres[where] = -out[l] if a == 0 else pres[where] - out[l]
             return carry
 
-        lax.fori_loop(0, order, diverge, 0)
-
-    arrive(round2)
+        lax.fori_loop(0, order, diverge, 0, unroll=True)
+
     for a in range(3):
+        arrive(round2[2 * a : 2 * a + 2])
         for s in range(2):
             up = s == 0
             edge = brick.edge(a, up)
@@ -518,13 +565,13 @@
                 total = rolled[0]
                 for k in range(1, order):
                     total = jnp.where(tile_of[k] == t, rolled[k], total)
-                rows_buf[0, i, t, pl.ds(j, brick.rows, stride=order), :] = permute(
+                rows_buf[i, 0, t, pl.ds(j, brick.rows, stride=order), :] = permute(
                     total, scatter_index
                 )
         for t in range(order):
             for x in range(ex):
                 smooth_ref[x * order + i, :, t * ez : (t + 1) * ez] = rows_buf[
-                    0, i, t, x * ny : (x + 1) * ny, :
+                    i, 0, t, x * ny : (x + 1) * ny, :
                 ]
         return carry
 
@@ -536,6 +583,7 @@
         total = total + recv3[n]
     for x in range(ex):
         coarse_ref[x] = total[x * ey : (x + 1) * ey]
+    finish(round1x)
     finish(round1)
     finish(round2)
     finish(round3)
@@ -555,33 +603,40 @@
         ]
 
     whole = pl.BlockSpec(memory_space=pltpu.VMEM)
+    remote = pl.BlockSpec(memory_space=pltpu.HBM)
     sems = pltpu.SemaphoreType.DMA
+    f32 = jnp.float32
+    layer = velocity.shape[2:]
     return pl.pallas_call(
         functools.partial(body, brick, counts),
         out_shape=(
-            jax.ShapeDtypeStruct(velocity.shape[1:], jnp.float32),
-            jax.ShapeDtypeStruct(mask.shape, jnp.float32),
+            jax.ShapeDtypeStruct(velocity.shape[1:], f32),
+            jax.ShapeDtypeStruct(mask.shape, f32),
         ),
-        in_specs=[whole] * 3,
+        in_specs=[remote] * 3,
         out_specs=(whole, whole),
         scratch_shapes=[
-            pltpu.VMEM((3, order, order, brick.rows * order, ez), jnp.float32),
-            pltpu.VMEM((3, order, order, order) + tile, jnp.float32),
-            pltpu.VMEM((3, order, order, order) + tile, jnp.float32),
-            pltpu.VMEM((3, order, order) + tile, jnp.float32),
-            pltpu.VMEM((order, order, order) + tile, jnp.float32),
+            pltpu.VMEM(velocity.shape, f32),
+            pltpu.VMEM(mask.shape, jnp.int32),
+            pltpu.VMEM(scale.shape, f32),
+            pltpu.VMEM((order, 3, order, brick.rows * order, ez), f32),
+            pltpu.VMEM((3, order, order, order) + tile, f32),
+            pltpu.VMEM((3, order, order, order) + tile, f32),
+            pltpu.VMEM((2, 3, order, order) + tile, f32),
+            pltpu.VMEM((3, order, order) + tile, f32),
+            pltpu.VMEM((order, order, order) + tile, f32),
+            pltpu.VMEM((2, 3) + layer, f32),
         ]
-        + buffers(3 * faces)
-        + buffers(3 * faces)
+        + buffers(3 * faces)[2:]
+        + buffers(3 * faces)[2:]
         + buffers(faces)
         + buffers(faces)
-        + [
-            pltpu.VMEM((len(corners),) + tile, jnp.float32),
-            pltpu.VMEM((len(corners),) + tile, jnp.float32),
-        ]
-        + [sems((6,)), sems((6,)), sems((6,)), sems((6,)), sems((7,)), sems((7,))],
+        + [pltpu.VMEM((len(corners),) + tile, f32)] * 2
+        + [sems((6,))] * 4
+        + [sems((len(corners),))] * 2
+        + [sems((ex * order,)), sems((2,)), sems((6,)), sems((6,))],
         compiler_params=pltpu.CompilerParams(
-            collective_id=0, has_side_effects=True, vmem_limit_bytes=40 * 2**20
+            collective_id=0, has_side_effects=True, vmem_limit_bytes=67043328
         ),
     )(velocity, mask, scale)
 

time: 21.7 us -> 20.8 us (0.959)
  local copies, waits for them, and re-layouts: 4.29 us -> 3.2 us
    unnamed x8 -> x2, local copies, waits for them, and re-layouts: 4.29 us -> 3.2 us
    pallas_call x1, Pallas kernels: 16.6 us -> 16.8 us  [shards(): pl.pallas_call(functools.partial(body, brick, counts), out_shape=(jax.Sha...]
where the time goes in v1:
time: 20.8 us; the launch traced here: 20.6 us
  Pallas kernels  16.8 us (81%)
  local copies, waits for them, and re-layouts  3.2 us (15%)
  between operations  0.64 us (3%)
    pallas_call x1, Pallas kernels, shards(): pl.pallas_call(functools.partial(body, brick, counts), out_shape=(jax.Sha...  16.8 us
    unnamed x2, local copies, waits for them, and re-layouts  3.2 us

profile of v1, /device:TPU:0, one launch (start us, length us, event | category | flops | bytes accessed | tf_op | source)
XLA Modules:
  0.0 20.6 jit_solution(2849262134833176264)
XLA Ops:
  0.6 16.8 %shard_map.50 = (f32[10,20,640]{2,1,0:T(8,128)}, f32[2,4,128]{2,1,0:T(4,128)}) custom-call(f32[3,10,20,640]{3,2,1,0:T(8,128)} %v_ref.1, s32[2,4,128]{2,1,0:T(4,128)} %mask_ref.1, f32[2,4,128]{2,1,0:T(4,128)} %scale_ref.1), custom_call_target="tpu_custom_call" | custom-call | tf_op jit(solution)/shard_map/pallas_call | solution.py:610
  17.4 1.9 %copy.7 = f32[10,20,640]{2,1,0:T(8,128)} copy(f32[10,20,640]{2,1,0:T(8,128)} %get-tuple-element.4) | data formatting | bytes 1024000
  19.4 1.3 %copy.8 = f32[2,4,128]{2,1,0:T(4,128)} copy(f32[2,4,128]{2,1,0:T(4,128)} %get-tuple-element.5) | data formatting | bytes 8192

commit v2 on v1

--- a/solution.py
+++ b/solution.py
@@ -346,9 +346,6 @@
                         total = jnp.where(tile_of[k] == t, parts[t], total)
                     put(c, j, k, roll(total, -spread * k, 1))
 
-    pl.semaphore_wait(barrier, sum(exists(shift).astype(jnp.int32) for shift in partners))
-    start(round1x)
-
     def split(i, carry):
         for x in range(ex):
             n = x * order + i
@@ -363,7 +360,10 @@
         split_layer({x: reader(x) for x in range(ex)}, rows_buf.at[i], put)
         return carry
 
-    lax.fori_loop(0, order, split, 0)
+    lax.fori_loop(0, 2, split, 0)
+    pl.semaphore_wait(barrier, sum(exists(shift).astype(jnp.int32) for shift in partners))
+    start(round1x)
+    lax.fori_loop(2, order, split, 0)
 
     clear(round1x)
     clear(round1)
@@ -470,6 +470,8 @@
             face = face_of(conv.at[a], a, l).reshape(faces, brick.rows, ez)
             send2[2 * a + s][...] = brick.pack(face, a, s == 0)
         start(round2[2 * a : 2 * a + 2])
+
+    for a in range(3):
 
         def diverge(m, carry):
             out = lifted_derivative([conv[(a,) + at_line(a, l, m)] for l in range(order)])
@@ -607,6 +609,7 @@
     sems = pltpu.SemaphoreType.DMA
     f32 = jnp.float32
     layer = velocity.shape[2:]
+    kept = 4 * velocity.size * 1 // 1
     return pl.pallas_call(
         functools.partial(body, brick, counts),
         out_shape=(
@@ -636,7 +639,7 @@
         + [sems((len(corners),))] * 2
         + [sems((ex * order,)), sems((2,)), sems((6,)), sems((6,))],
         compiler_params=pltpu.CompilerParams(
-            collective_id=0, has_side_effects=True, vmem_limit_bytes=67043328
+            collective_id=0, has_side_effects=True, vmem_limit_bytes=67043328 - kept
         ),
     )(velocity, mask, scale)
 

time: 20.8 us -> 20.4 us (0.981)
  Pallas kernels: 16.8 us -> 16.4 us
    pallas_call x1, Pallas kernels: 16.8 us -> 16.4 us  [shards(): pl.pallas_call(functools.partial(body, brick, counts), out_shape=(jax.Sha...]
where the time goes in v2:
time: 20.4 us; the launch traced here: 20.2 us
  Pallas kernels  16.4 us (80%)
  local copies, waits for them, and re-layouts  3.2 us (16%)
  between operations  0.64 us (3%)
    pallas_call x1, Pallas kernels, shards(): pl.pallas_call(functools.partial(body, brick, counts), out_shape=(jax.Sha...  16.4 us
    unnamed x2, local copies, waits for them, and re-layouts  3.2 us

profile of v2, /device:TPU:0, one launch (start us, length us, event | category | flops | bytes accessed | tf_op | source)
XLA Modules:
  0.0 20.2 jit_solution(5304225303719863893)
XLA Ops:
  0.6 16.4 %shard_map.50 = (f32[10,20,640]{2,1,0:T(8,128)}, f32[2,4,128]{2,1,0:T(4,128)}) custom-call(f32[3,10,20,640]{3,2,1,0:T(8,128)} %v_ref.1, s32[2,4,128]{2,1,0:T(4,128)} %mask_ref.1, f32[2,4,128]{2,1,0:T(4,128)} %scale_ref.1), custom_call_target="tpu_custom_call" | custom-call | tf_op jit(solution)/shard_map/pallas_call | solution.py:613
  17.0 1.9 %copy.7 = f32[10,20,640]{2,1,0:T(8,128)} copy(f32[10,20,640]{2,1,0:T(8,128)} %get-tuple-element.4) | data formatting | bytes 1024000
  18.9 1.3 %copy.8 = f32[2,4,128]{2,1,0:T(4,128)} copy(f32[2,4,128]{2,1,0:T(4,128)} %get-tuple-element.5) | data formatting | bytes 8192
